TPU v7x, 128 devices: a whole 4x4x4 slice. The times are simulated.
128 devices in a mesh: seq: 32 (over y, x, core), tp: 4 (over z).
Axes of the slice: x: 4, y: 4, z: 4, core: 2. Of those that a mesh axis runs over, the one named last changes fastest.
Arguments:
- codes: bfloat16 [16384, 4096], P('seq', 'tp'), may hold values from -127 to 127, as said below
- exponents: int32 [16384], P('seq'), may hold values from -8 to -5
- w_query: bfloat16 [4096, 4096], P(None, 'tp'), may hold values from -0.09375 to 0.09375
- w_key: bfloat16 [4096, 4096], P(None, 'tp'), may hold values from -0.09375 to 0.09375
- w_value: bfloat16 [4096, 4096], P(None, 'tp'), may hold values from -0.09375 to 0.09375
- norm_gain: float32 [4096], P('tp'), may hold values from 0.1 to 1.9
- w_out: bfloat16 [4096, 4096], P('tp'), may hold values from -0.09375 to 0.09375
Outputs:
- mixed: bfloat16 [16384, 4096], P(('seq', 'tp'))
Inputs may be any that keep to these rules, and one draw needn't show every extreme that they name: `codes`: every entry is a whole number.
All inputs are finite; a program needn't handle non-finite values.
Results may differ from a plain program's by a relative error of at most 0.012.
Values may be sent and summed in bfloat16 or wider, within the bound.
No kernel may reach another device: no remote copies, remote signals or barrier semaphores. Data moves between devices by JAX's collectives and lax.ppermute only.
A program may use at most 128 MiB of HBM per device.

v0:
```python
import jax
import jax.numpy as jnp
from jax import lax
from jax.sharding import PartitionSpec as P

HD = 128
BLK = 512


def prefix(x, axis, combine, identity):
    length, place = (lax.axis_size(axis), lax.axis_index(axis))
    everything = lax.all_gather(x, axis)
    start = jnp.broadcast_to(jnp.asarray(identity, x.dtype), x.shape)

    def step(k, before):
        reached = k < place
        new = combine(before, everything[k])
        return jnp.where(reached, new, before)

    return lax.fori_loop(0, length, step, start)


def on_device(codes, exponents, w_query, w_key, w_value, norm_gain, w_out):
    tok_count = codes.shape[0]
    local_width = w_query.shape[1]
    heads_local = local_width // HD
    blocks = tok_count // BLK
    row_scale = jnp.exp2(exponents.astype(jnp.float32))[:, None]
    weights = (w_query, w_key, w_value)
    piece = lax.all_gather(codes, "tp", axis=1, tiled=True)
    query, keys, values = tuple(
        (jnp.dot(piece, weight, preferred_element_type=jnp.float32) for weight in weights)
    )
    feat_q = (
        (jax.nn.elu(query * row_scale) + 1.0)
        .astype(jnp.bfloat16)
        .reshape(blocks, BLK, heads_local, HD)
    )
    feat_k = (
        (jax.nn.elu(keys * row_scale) + 1.0)
        .astype(jnp.bfloat16)
        .reshape(blocks, BLK, heads_local, HD)
    )
    value_b = (values * row_scale).astype(jnp.bfloat16).reshape(blocks, BLK, heads_local, HD)
    block_states = jnp.einsum(
        "bshd,bshe->bhde", feat_k, value_b, preferred_element_type=jnp.float32
    )
    shard_state = jnp.sum(block_states, axis=0)
    zero_state = jnp.zeros((heads_local, HD, HD), jnp.float32)
    before = prefix(shard_state, "seq", lambda earlier, later: earlier + later, zero_state)
    states = (before[None] + (jnp.cumsum(block_states, axis=0) - block_states)).astype(jnp.bfloat16)
    inter = jnp.einsum("bshd,bhde->bshe", feat_q, states, preferred_element_type=jnp.float32)
    causal = jnp.tril(jnp.ones((BLK, BLK), jnp.float32))
    scores = jnp.einsum("bshd,bthd->bhst", feat_q, feat_k, preferred_element_type=jnp.float32)
    scores = (scores * causal[None, None]).astype(jnp.bfloat16)
    intra = jnp.einsum("bhst,bthe->bshe", scores, value_b, preferred_element_type=jnp.float32)
    summed = inter + intra
    mean_sq = jnp.mean(summed * summed, axis=-1, keepdims=True)
    gain = norm_gain.reshape(heads_local, HD)
    normed = (
        (summed * lax.rsqrt(mean_sq + 1e-05) * gain)
        .astype(jnp.bfloat16)
        .reshape(tok_count, local_width)
    )
    return lax.psum_scatter(
        jnp.dot(normed, w_out, preferred_element_type=jnp.float32).astype(jnp.bfloat16),
        "tp",
        scatter_dimension=0,
        tiled=True,
    )


def solution(mesh):
    in_specs = (
        P("seq", "tp"),
        P("seq"),
        P(None, "tp"),
        P(None, "tp"),
        P(None, "tp"),
        P("tp"),
        P("tp", None),
    )
    out_specs = P(("seq", "tp"), None)
    return jax.shard_map(
        on_device, mesh=mesh, in_specs=in_specs, out_specs=out_specs, check_vma=False
    )
```

profile of v0, /device:TPU:1, one launch (start us, length us, event | category | flops | bytes accessed | tf_op | source)
XLA Modules:
  0.0 268.6 jit_solution(1697507522976406608)
XLA Ops:
  8.0 52.5 %all-gather.4.cloned.1.call-done = bf16[512,4096]{1,0:T(8,128)(2,1)} async-done(((bf16[512,1024]{1,0:T(8,128)(2,1)}), bf16[512,4096]{1,0:T(8,128)(2,1)}) %all-gather.4.cloned.1.call-update) | async-done | bytes 4194320 | tf_op jit(solution)/shard_map/all_gather | solution.py:30
  60.5 9.8 %fusion.6 = bf16[512,1024]{1,0:T(8,128)(2,1)S(1)} fusion(bf16[512,4096]{1,0:T(8,128)(2,1)} %all-gather.4.cloned.1.call-done, bf16[4096,1024]{1,0:T(8,128)(2,1)} %param.12, f32[512]{0:T(512)S(1)} %multiply_exponential_fusion), kind=kOutput, calls=%fused_computation.12 | convolution fusion | flops 4298113024 | bytes 13633536 | tf_op jit(solution)/shard_map/dot_general | solution.py:32
  70.9 9.1 %multiply_convert_fusion.2 = bf16[512,1024]{1,0:T(8,128)(2,1)S(1)} fusion(bf16[512,4096]{1,0:T(8,128)(2,1)} %all-gather.4.cloned.1.call-done, bf16[4096,1024]{1,0:T(8,128)(2,1)} %param.13, f32[512]{0:T(512)S(1)} %multiply_exponential_fusion), kind=kOutput, calls=%fused_computation.21 | convolution fusion | flops 4296015872 | bytes 13633536 | tf_op jit(solution)/shard_map/dot_general | solution.py:32
  80.6 1.2 fusion.25
  83.2 10.8 %fusion.14 = bf16[64,8,8,128]{3,2,1,0:T(8,128)(2,1)} fusion(bf16[512,4096]{1,0:T(8,128)(2,1)} %all-gather.4.cloned.1.call-done, bf16[4096,1024]{1,0:T(8,128)(2,1)} %param.11, f32[512]{0:T(512)S(1)} %multiply_exponential_fusion), kind=kOutput, calls=%fused_computation.23 | convolution fusion | flops 4298113024 | bytes 13633536 | tf_op jit(solution)/shard_map/dot_general | solution.py:32
  94.0 61.2 %all-gather.6.cloned.1.call-done = f32[256,128,128]{2,1,0:T(8,128)} async-done(((f32[8,128,128]{2,1,0:T(8,128)}), f32[256,128,128]{2,1,0:T(8,128)}) %all-gather.6.cloned.1.call-update) | async-done | bytes 16777232 | tf_op jit(solution)/shard_map/all_gather | solution.py:12
  155.1 40.0 %while.14 = (s32[]{:T(128)}, f32[8,128,128]{2,1,0:T(8,128)S(1)}, s32[]{:T(128)}, f32[32,8,128,128]{3,2,1,0:T(8,128)}, s32[]{:T(128)}, /*index=5*/s32[]{:T(128)}) while((s32[]{:T(128)}, f32[8,128,128]{2,1,0:T(8,128)S(1)}, s32[]{:T(128)}, f32[32,8,128,128]{3,2,1,0:T(8,128)}, s32[]{:T(128)}, /*index=5*/s32[]{:T(128)}) %tuple.42), condition=%wide.region_1.2_spmd.clone, body=%wide.region_0.1_spmd.clone.sunk | while | flops 393220 | bytes 1572965 | solution.py:20
  156.4 1.2 add_select_fusion.2
  157.6 1.2 add_select_fusion.2
  158.9 1.2 add_select_fusion.2
  160.1 1.2 add_select_fusion.2
  161.4 1.2 add_select_fusion.2
  162.6 1.2 add_select_fusion.2
  163.9 1.2 add_select_fusion.2
  165.2 1.2 add_select_fusion.2
  166.4 1.2 add_select_fusion.2
  167.7 1.2 add_select_fusion.2
  168.9 1.2 add_select_fusion.2
  170.2 1.2 add_select_fusion.2
  171.4 1.2 add_select_fusion.2
  172.7 1.2 add_select_fusion.2
  173.9 1.2 add_select_fusion.2
  175.2 1.2 add_select_fusion.2
  176.4 1.2 add_select_fusion.2
  177.7 1.2 add_select_fusion.2
  183.9 1.2 add_select_fusion.2
  193.9 1.2 add_select_fusion.2
  195.2 3.1 %fusion.17 = f32[8,128,512]{2,1,0:T(8,128)} fusion(bf16[64,8,8,128]{3,2,1,0:T(8,128)(2,1)} %fusion.14, f32[8,128,128]{2,1,0:T(8,128)S(1)} %get-tuple-element.84, f32[8,128,128]{2,1,0:T(8,128)S(1)} %copy-done), kind=kOutput, calls=%fused_computation.25 | convolution fusion | flops 134610944 | bytes 4194304 | tf_op jit(solution)/shard_map/bshd,bhde->bshe/dot_general | solution.py:52
  198.2 6.1 %fusion.10 = (f32[512,8]{0,1:T(8,128)S(1)}, f32[8,128,512]{2,1,0:T(8,128)}) fusion(f32[8,128,512]{2,1,0:T(8,128)} %fusion.17, bf16[512,8,128]{0,2,1:T(8,128)(2,1)S(1)} %bitcast.45, f32[512,512]{1,0:T(8,128)} %fusion.19, bf16[512,8,128]{0,2,1:T(8,128)(2,1)S(1)} %bitcast.43, bf16[64,8,8,128]{3,2,1,0:T(8,128)(2,1)} %fusion.14), kind=kOutput, calls=%fused_computation.18 | convolution fusion | flops 1079504896 | bytes 8404992 | tf_op jit(solution)/shard_map/bhst,bthe->bshe/dot_general | solution.py:56
  204.4 1.9 fusion.12
  206.3 9.5 %convolution_convert_fusion = bf16[512,4096]{1,0:T(8,128)(2,1)} fusion(bf16[512,1024]{0,1:T(8,128)(2,1)S(1)} %bitcast.46, bf16[1024,4096]{1,0:T(8,128)(2,1)} %param.15), kind=kOutput, calls=%fused_computation.6 | convolution fusion | flops 4297064448 | bytes 13631488 | tf_op jit(solution)/shard_map/dot_general | solution.py:66
  215.8 46.3 %reduce-scatter.2.cloned.1.call-done = bf16[128,4096]{1,0:T(8,128)(2,1)} async-done(((bf16[512,4096]{1,0:T(8,128)(2,1)}), bf16[128,4096]{1,0:T(8,128)(2,1)}) %reduce-scatter.2.cloned.1.call-update) | async-done | bytes 1048592 | tf_op jit(solution)/shard_map/reduce_scatter | solution.py:65
  (28 shorter events, 18.6 us)
Async XLA Ops:
  6.5 53.9 %all-gather.4.cloned.1.call-start = ((), (), s32[]{:S(2)}) async-start(), calls=%async_computation.1 | async-start | bytes 5242880 | tf_op jit(solution)/shard_map/all_gather | solution.py:30
  7.3 147.9 %all-gather.6.cloned.1.call-start = ((), (), s32[]{:S(2)}) async-start(), calls=%async_computation.3 | async-start | bytes 17301504 | tf_op jit(solution)/shard_map/all_gather | solution.py:12
  81.8 180.2 %reduce-scatter.2.cloned.1.call-start = ((), (), s32[]{:S(2)}) async-start(), calls=%async_computation.2 | async-start | bytes 5242880 | tf_op jit(solution)/shard_map/reduce_scatter | solution.py:65
  94.0 101.2 %copy-start = (f32[8,128,128]{2,1,0:T(8,128)S(1)}, f32[8,128,128]{2,1,0:T(8,128)}, u32[]{:S(2)}) copy-start(f32[8,128,128]{2,1,0:T(8,128)} %fusion.25) | copy-start | bytes 1572868
  198.2 6.1 %copy-start.1 = (f32[1024]{0:T(1024)S(1)}, f32[1024]{0:T(1024)}, u32[]{:S(2)}) copy-start(f32[1024]{0:T(1024)} %param.14) | copy-start | bytes 12292
Sparse Core Ops, SparseCore 0:
  9.0 51.4 all-gather.3
  82.0 73.1 all-gather.5
  215.9 46.0 reduce-scatter.1
where the time goes:
time: 270 us; the launch traced here: 269 us
  waiting for transfers between devices  161 us (60%)
  matrix products  49.7 us (18%)
  other arithmetic  42.9 us (16%)
  between operations  13.2 us (5%)
    all_gather x1, waiting for transfers between devices, prefix(): everything = lax.all_gather(x, axis)  61.2 us
    all_gather x1, waiting for transfers between devices, on_device(): piece = lax.all_gather(codes, 'tp', axis=1, tiled=True)  52.5 us
    reduce_scatter x1, waiting for transfers between devices, on_device(): lax.psum_scatter(jnp.dot(normed, w_out, preferred_element_type=jnp.float3...  46.3 us
    select_n x32, other arithmetic, step(): return jnp.where(reached, new, before)  39.3 us
    dot_general x3, matrix products, on_device(): jnp.dot(piece, weight, preferred_element_type=jnp.float32)  29.8 us
    dot_general x1, matrix products, on_device(): jnp.dot(normed, w_out, preferred_element_type=jnp.float32)  9.5 us
    dot_general x1, matrix products, on_device(): jnp.einsum('bhst,bthe->bshe', scores, value_b, preferred_element_type=jnp...  6.13 us
  transfers between devices with their start and end apart: 3, of which 3 were waited for; matrix products, arithmetic and copies ran while one was open for 5% of the time, Pallas kernels for 0%

commit v1 on v0

--- a/solution.py
+++ b/solution.py
@@ -5,6 +5,12 @@
 
 HD = 128
 BLK = 512
+
+
+def joined_along(blocks, dim):
+    lengths = list(blocks.shape[1:])
+    lengths[dim] *= blocks.shape[0]
+    return jnp.moveaxis(blocks, 0, dim).reshape(lengths)
 
 
 def prefix(x, axis, combine, identity):
@@ -27,7 +33,19 @@
     blocks = tok_count // BLK
     row_scale = jnp.exp2(exponents.astype(jnp.float32))[:, None]
     weights = (w_query, w_key, w_value)
-    piece = lax.all_gather(codes, "tp", axis=1, tiled=True)
+    length_2 = lax.axis_size("tp")
+    pairs = [(i, (i + 1) % length_2) for i in range(length_2)]
+    back = [(b, a) for a, b in pairs]
+    lower, upper = ([], [])
+    for step_2 in range(length_2 - 1):
+        if step_2 % 2 == 0:
+            lower.append(lax.ppermute(lower[-1] if lower else codes, "tp", pairs))
+        else:
+            upper.append(lax.ppermute(upper[-1] if upper else codes, "tp", back))
+    parts = jnp.stack([*lower[::-1], codes, *upper])
+    shift = lax.axis_index("tp") - len(lower)
+    parts = parts[(jnp.arange(length_2) - shift) % length_2]
+    piece = joined_along(parts, 1)
     query, keys, values = tuple(
         (jnp.dot(piece, weight, preferred_element_type=jnp.float32) for weight in weights)
     )

time: 270 us -> 280 us (1.037)
  local copies, waits for them, and re-layouts: 1.09 us -> 12.7 us
  waiting for transfers between devices: 161 us -> 155 us
  starting transfers between devices: 0.26 us -> 4.8 us
  matrix products: 49.7 us -> 46.7 us
    all_gather x1 -> x0, waiting for transfers between devices: 52.5 us -> none  [on_device(): piece = lax.all_gather(codes, 'tp', axis=1, tiled=True)]
    ppermute x0 -> x3, waiting for transfers between devices: none -> 47 us  [the longest x2 47 us: on_device(): lower.append(lax.ppermute(lower[-1] if lower else codes, 'tp', pairs))]
    transpose x0 -> x1, local copies, waits for them, and re-layouts: none -> 6.2 us  [joined_along(): return jnp.moveaxis(blocks, 0, dim).reshape(lengths)]
    gather x0 -> x1, local copies, waits for them, and re-layouts: none -> 4.95 us  [on_device(): parts = parts[(jnp.arange(length_2) - shift) % length_2]]
    ppermute x0 -> x3, starting transfers between devices: none -> 4.58 us  [the longest x2 2.46 us: on_device(): lower.append(lax.ppermute(lower[-1] if lower else codes, 'tp', pairs))]
    another operation x0 -> x1, other arithmetic: none -> 3.28 us  [on_device(): parts = jnp.stack([*lower[::-1], codes, *upper])]
  transfers between devices with their start and end apart: 3 -> 5, of which waited for: 3 -> 4; matrix products, arithmetic and copies ran while one was open for 5% -> 4% of each run, Pallas kernels for 0% -> 0%
where the time goes in v1:
time: 280 us; the launch traced here: 279 us
  waiting for transfers between devices  155 us (55%)
  matrix products  46.7 us (17%)
  other arithmetic  44.6 us (16%)
  between operations  13.5 us (5%)
  local copies, waits for them, and re-layouts  12.7 us (5%)
  starting transfers between devices  4.8 us (2%)
    all_gather x1, waiting for transfers between devices, prefix(): everything = lax.all_gather(x, axis)  62.1 us
    ppermute x2, waiting for transfers between devices, on_device(): lower.append(lax.ppermute(lower[-1] if lower else codes, 'tp', pairs))  47 us
    reduce_scatter x1, waiting for transfers between devices, on_device(): lax.psum_scatter(jnp.dot(normed, w_out, preferred_element_type=jnp.float3...  46.3 us
    select_n x32, other arithmetic, step(): return jnp.where(reached, new, before)  39.3 us
    dot_general x3, matrix products, on_device(): jnp.dot(piece, weight, preferred_element_type=jnp.float32)  28.9 us
    dot_general x1, matrix products, on_device(): jnp.dot(normed, w_out, preferred_element_type=jnp.float32)  9.51 us
    transpose x1, local copies, waits for them, and re-layouts, joined_along(): return jnp.moveaxis(blocks, 0, dim).reshape(lengths)  6.2 us
  transfers between devices with their start and end apart: 5, of which 4 were waited for; matrix products, arithmetic and copies ran while one was open for 4% of the time, Pallas kernels for 0%

profile of v1, /device:TPU:1, one launch (start us, length us, event | category | flops | bytes accessed | tf_op | source)
XLA Modules:
  0.0 278.5 jit_solution(12882523355125753035)
XLA Ops:
  6.5 2.5 collective-permute-start
  9.0 2.1 collective-permute-start.2
  11.1 23.1 %collective-permute-done = bf16[512,1024]{1,0:T(8,128)(2,1)S(1)} collective-permute-done((bf16[512,1024]{1,0:T(8,128)(2,1)}, bf16[512,1024]{1,0:T(8,128)(2,1)S(1)}, u32[]{:S(2)}, u32[]{:S(2)}) %collective-permute-start) | collective-permute-done | bytes 1048608 | tf_op jit(solution)/shard_map/ppermute | solution.py:42
  34.9 24.0 %collective-permute-done.1 = bf16[512,1024]{1,0:T(8,128)(2,1)S(1)} collective-permute-done((bf16[512,1024]{1,0:T(8,128)(2,1)S(1)}, bf16[512,1024]{1,0:T(8,128)(2,1)S(1)}, u32[]{:S(2)}, u32[]{:S(2)}) %collective-permute-start.1) | collective-permute-done | bytes 1048608 | tf_op jit(solution)/shard_map/ppermute | solution.py:42
  58.9 3.3 %pad_maximum_fusion = bf16[4,512,1024]{2,1,0:T(8,128)(2,1)} fusion(bf16[1,512,1024]{2,1,0:T(8,128)(2,1)S(1)} %bitcast.66, bf16[1,512,1024]{2,1,0:T(8,128)(2,1)} %bitcast.64, bf16[1,512,1024]{2,1,0:T(8,128)(2,1)S(1)} %bitcast.65, bf16[1,512,1024]{2,1,0:T(8,128)(2,1)S(1)} %bitcast.67), kind=kLoop, calls=%fused_computation.9 | loop fusion | flops 6291456 | bytes 8388608 | tf_op jit(solution)/shard_map/stack | solution.py:45
  62.1 4.9 %gather_fusion = bf16[4,512,1024]{2,1,0:T(8,128)(2,1)} fusion(bf16[4,512,1024]{2,1,0:T(8,128)(2,1)} %pad_maximum_fusion, s32[1024]{0:T(1024)S(1)} %pad_clamp_fusion), kind=kCustom, calls=%fused_computation | custom fusion | bytes 8388624 | tf_op jit(solution)/shard_map/gather | solution.py:47
  67.1 6.2 %copy.26 = bf16[512,4,1024]{0,2,1:T(8,128)(2,1)} copy(bf16[512,4,1024]{2,0,1:T(8,128)(2,1)} %bitcast.57) | data formatting | bytes 8388608 | tf_op jit(solution)/shard_map/transpose | solution.py:13
  73.3 9.2 %multiply_convert_fusion.2 = bf16[512,1024]{1,0:T(8,128)(2,1)S(1)} fusion(bf16[512,4096]{0,1:T(8,128)(2,1)} %bitcast.58, bf16[4096,1024]{1,0:T(8,128)(2,1)} %param.13, f32[512]{0:T(512)S(1)} %multiply_exponential_fusion), kind=kOutput, calls=%fused_computation.23 | convolution fusion | flops 4296015872 | bytes 13633536 | tf_op jit(solution)/shard_map/dot_general | solution.py:50
  83.0 9.9 %fusion.15 = bf16[64,8,8,128]{3,2,1,0:T(8,128)(2,1)S(1)} fusion(bf16[512,4096]{0,1:T(8,128)(2,1)} %bitcast.59, bf16[4096,1024]{1,0:T(8,128)(2,1)} %param.12, f32[512]{0:T(512)S(1)} %multiply_exponential_fusion), kind=kOutput, calls=%fused_computation.26 | convolution fusion | flops 4298113024 | bytes 13633536 | tf_op jit(solution)/shard_map/dot_general | solution.py:50
  93.8 1.3 fusion.20
  96.5 9.9 %fusion.14 = bf16[64,8,8,128]{3,2,1,0:T(8,128)(2,1)S(1)} fusion(bf16[512,4096]{0,1:T(8,128)(2,1)} %bitcast.60, bf16[4096,1024]{1,0:T(8,128)(2,1)} %param.11, f32[512]{0:T(512)S(1)} %multiply_exponential_fusion), kind=kOutput, calls=%fused_computation.25 | convolution fusion | flops 4298113024 | bytes 13633536 | tf_op jit(solution)/shard_map/dot_general | solution.py:50
  106.4 62.1 %all-gather.3.cloned.1.call-done = f32[256,128,128]{2,1,0:T(8,128)} async-done(((f32[8,128,128]{2,1,0:T(8,128)}), f32[256,128,128]{2,1,0:T(8,128)}) %all-gather.3.cloned.1.call-update) | async-done | bytes 16777232 | tf_op jit(solution)/shard_map/all_gather | solution.py:18
  168.5 40.0 %while.14 = (s32[]{:T(128)}, f32[8,128,128]{2,1,0:T(8,128)S(1)}, s32[]{:T(128)}, f32[32,8,128,128]{3,2,1,0:T(8,128)}, s32[]{:T(128)}, /*index=5*/s32[]{:T(128)}) while((s32[]{:T(128)}, f32[8,128,128]{2,1,0:T(8,128)S(1)}, s32[]{:T(128)}, f32[32,8,128,128]{3,2,1,0:T(8,128)}, s32[]{:T(128)}, /*index=5*/s32[]{:T(128)}) %tuple.40), condition=%wide.region_1.2_spmd.clone, body=%wide.region_0.1_spmd.clone.sunk | while | flops 393220 | bytes 1572965 | solution.py:26
  169.8 1.2 add_select_fusion.2
  171.0 1.2 add_select_fusion.2
  172.3 1.2 add_select_fusion.2
  173.5 1.2 add_select_fusion.2
  174.8 1.2 add_select_fusion.2
  176.0 1.2 add_select_fusion.2
  177.3 1.2 add_select_fusion.2
  178.5 1.2 add_select_fusion.2
  179.8 1.2 add_select_fusion.2
  181.0 1.2 add_select_fusion.2
  182.3 1.2 add_select_fusion.2
  183.5 1.2 add_select_fusion.2
  184.8 1.2 add_select_fusion.2
  186.0 1.2 add_select_fusion.2
  199.8 1.2 add_select_fusion.2
  208.6 1.8 fusion.18
  210.4 5.1 %fusion.10 = (f32[512,8]{0,1:T(8,128)S(1)}, f32[8,128,512]{2,1,0:T(8,128)S(1)}) fusion(f32[8,128,512]{2,1,0:T(8,128)} %fusion.18, bf16[512,8,128]{0,2,1:T(8,128)(2,1)S(1)} %bitcast.62, f32[512,512]{1,0:T(8,128)} %fusion.24, bf16[64,8,8,128]{3,2,1,0:T(8,128)(2,1)} %copy-done.2, bf16[64,8,8,128]{3,2,1,0:T(8,128)(2,1)} %copy-done.1), kind=kOutput, calls=%fused_computation.20 | convolution fusion | flops 1079504896 | bytes 8404992 | tf_op jit(solution)/shard_map/bhst,bthe->bshe/dot_general | solution.py:74
  215.9 9.5 %convolution_convert_fusion = bf16[512,4096]{1,0:T(8,128)(2,1)} fusion(bf16[512,1024]{0,1:T(8,128)(2,1)S(1)} %bitcast.63, bf16[1024,4096]{1,0:T(8,128)(2,1)} %param.15), kind=kOutput, calls=%fused_computation.7 | convolution fusion | flops 4297064448 | bytes 13631488 | tf_op jit(solution)/shard_map/dot_general | solution.py:84
  225.4 46.3 %reduce-scatter.2.cloned.1.call-done = bf16[128,4096]{1,0:T(8,128)(2,1)} async-done(((bf16[512,4096]{1,0:T(8,128)(2,1)}), bf16[128,4096]{1,0:T(8,128)(2,1)}) %reduce-scatter.2.cloned.1.call-update) | async-done | bytes 1048592 | tf_op jit(solution)/shard_map/reduce_scatter | solution.py:83
  (39 shorter events, 24.7 us)
Async XLA Ops:
  6.5 162.0 %all-gather.3.cloned.1.call-start = ((), (), s32[]{:S(2)}) async-start(), calls=%async_computation.2 | async-start | bytes 17301504 | tf_op jit(solution)/shard_map/all_gather | solution.py:18
  6.5 27.6 %collective-permute-start = (bf16[512,1024]{1,0:T(8,128)(2,1)}, bf16[512,1024]{1,0:T(8,128)(2,1)S(1)}, u32[]{:S(2)}, u32[]{:S(2)}) collective-permute-start(bf16[512,1024]{1,0:T(8,128)(2,1)} %param.9), channel_id=1, source_target_pairs={{0,1},{1,2},{2,3},{3,0},{4,5},{5,6},{6,7},{7,4},{8,9},{9,10},{10,1... | collective-permute-start | bytes 3145736 | tf_op jit(solution)/shard_map/ppermute | solution.py:42
  9.0 25.9 %collective-permute-start.2 = (bf16[512,1024]{1,0:T(8,128)(2,1)}, bf16[512,1024]{1,0:T(8,128)(2,1)S(1)}, u32[]{:S(2)}, u32[]{:S(2)}) collective-permute-start(bf16[512,1024]{1,0:T(8,128)(2,1)} %param.9), channel_id=1, source_target_pairs={{1,0},{2,1},{3,2},{0,3},{5,4},{6,5},{7,6},{4,7},{9,8},{10,9},{11,1... | collective-permute-start | bytes 3145736 | tf_op jit(solution)/shard_map/ppermute | solution.py:44
  34.2 24.7 %collective-permute-start.1 = (bf16[512,1024]{1,0:T(8,128)(2,1)S(1)}, bf16[512,1024]{1,0:T(8,128)(2,1)S(1)}, u32[]{:S(2)}, u32[]{:S(2)}) collective-permute-start(bf16[512,1024]{1,0:T(8,128)(2,1)S(1)} %collective-permute-done), channel_id=1, source_target_pairs={{0,1},{1,2},{2,3},{3,0},{4,5},{5,6},{6,7},{7,4},{8,9},{9,10},{10,1... | collective-permute-start | bytes 3145736 | tf_op jit(solution)/shard_map/ppermute | solution.py:42
  92.9 1.0 copy-start.1
  95.2 176.5 %reduce-scatter.2.cloned.1.call-start = ((), (), s32[]{:S(2)}) async-start(), calls=%async_computation.1 | async-start | bytes 5242880 | tf_op jit(solution)/shard_map/reduce_scatter | solution.py:83
  106.4 102.1 %copy-start.2 = (bf16[64,8,8,128]{3,2,1,0:T(8,128)(2,1)}, bf16[64,8,8,128]{3,2,1,0:T(8,128)(2,1)S(1)}, u32[]{:S(2)}) copy-start(bf16[64,8,8,128]{3,2,1,0:T(8,128)(2,1)S(1)} %fusion.14) | copy-start | bytes 3145732
  106.4 102.1 %copy-start = (f32[8,128,128]{2,1,0:T(8,128)S(1)}, f32[8,128,128]{2,1,0:T(8,128)}, u32[]{:S(2)}) copy-start(f32[8,128,128]{2,1,0:T(8,128)} %fusion.20) | copy-start | bytes 1572868
  210.4 5.2 %copy-start.3 = (f32[1024]{0:T(1024)S(1)}, f32[1024]{0:T(1024)}, u32[]{:S(2)}) copy-start(f32[1024]{0:T(1024)} %param.14) | copy-start | bytes 12292
Sparse Core Ops, SparseCore 0:
  95.3 73.1 all-gather.2
  225.5 46.1 reduce-scatter.1
